TPU v7x, 32 devices: a whole 2x2x4 slice. The times are simulated.
32 devices in a mesh: dp: 4 (over x, core), cls: 8 (over z, y).
Axes of the slice: x: 2, y: 2, z: 4, core: 2. Of those that a mesh axis runs over, the one named last changes fastest.
Arguments:
- faces: bfloat16 [2, 32, 512], P(None, ('dp', 'cls')), may hold values from -2 to 2
- labels: int32 [2, 32], replicated, may hold values from 0 to 16383, as said below
- centres: bfloat16 [16384, 512], P(('dp', 'cls')), may hold values from -4 to 4
- momentum: bfloat16 [16384, 512], P(('dp', 'cls')), may hold values from -3 to 3
Outputs:
- face_grad: float32 [2, 32, 512], P(None, ('dp', 'cls'))
- new_centres: bfloat16 [16384, 512], P(('dp', 'cls'))
- new_momentum: bfloat16 [16384, 512], P(('dp', 'cls'))
Inputs may be any that keep to these rules, and one draw needn't show every extreme that they name: `labels`: some face has class 0 and some face has class 16384 - 1.
All inputs are finite; a program needn't handle non-finite values.
Results may differ from a plain program's by a relative error of at most 0.0057.
Values may be sent and summed in bfloat16 or wider, within the bound.
A program may use at most 64 MiB of HBM per device.

v0:
```python
import jax
import jax.numpy as jnp
from jax import lax
from jax.sharding import PartitionSpec as P

SCALE = 30.0
MARGIN = 0.4
POS_WEIGHT = 0.7
BIAS = 6.5
EPS = 1e-06
MOMENTUM_RATE = 0.9
LEARN_RATE = 0.1
DECAY = 0.0005


def as_sent(x):

    def short(part):
        return part.astype(jnp.bfloat16) if part.dtype == jnp.float32 else part

    return jax.tree.map(short, x)


def logit_grad(cosine, positive):
    halfway = (cosine + 1.0) * 0.5
    shaped = 2.0 * halfway * halfway * halfway - 1.0
    slopes = 3.0 * halfway * halfway
    pos_term = -POS_WEIGHT * SCALE * jax.nn.sigmoid(-(SCALE * (shaped - MARGIN) + BIAS))
    neg_term = (1.0 - POS_WEIGHT) * SCALE * jax.nn.sigmoid(SCALE * (shaped + MARGIN) + BIAS)
    return (jnp.where(positive, pos_term, neg_term) * slopes).astype(jnp.bfloat16)


def normalize(centres):
    master = centres.astype(jnp.float32)
    length = jnp.sqrt(jnp.sum(master * master, axis=1, keepdims=True) + EPS)
    return (master, length, master / length)


def update(master, length, unit_wide, grad_unit, momentum):
    radial = jnp.sum(unit_wide * grad_unit, axis=1, keepdims=True)
    grad_centre = (grad_unit - unit_wide * radial) / length
    velocity = MOMENTUM_RATE * momentum.astype(jnp.float32) + grad_centre + DECAY * master
    return ((master - LEARN_RATE * velocity).astype(jnp.bfloat16), velocity.astype(jnp.bfloat16))


def fold_faces(pieces, folder, start_carry):
    grouped = jax.tree.map(
        lambda part, own: part.astype(own.dtype),
        lax.all_gather(as_sent(pieces), "cls", axis=0, tiled=True),
        pieces,
    )
    return folder(
        start_carry,
        jax.tree.map(lambda part: lax.all_gather(part, "dp", axis=0, tiled=True), as_sent(grouped)),
        jnp.int32(0),
    )


def spread_back(term, face_rows):
    group_rows = lax.psum_scatter(
        term(jnp.int32(0), face_rows * lax.axis_size("cls") * lax.axis_size("dp")).astype(
            jnp.bfloat16
        ),
        "dp",
        scatter_dimension=0,
        tiled=True,
    ).astype(jnp.float32)
    return lax.psum_scatter(group_rows, "cls", scatter_dimension=0, tiled=True)


def local(faces, labels, centres, momentum):
    cls_rows = centres.shape[0]
    width = centres.shape[1]
    batches = faces.shape[0]
    face_rows = faces.shape[1]
    total_rows = labels.shape[1]
    master, length, unit_wide = normalize(centres)
    unit_rows = unit_wide.astype(jnp.bfloat16)
    class_ids = lax.axis_index(("dp", "cls")) * cls_rows + jnp.arange(cls_rows, dtype=jnp.int32)

    def make_fold(label_sets):

        def folder(carry, pieces, start):
            grad_unit, slope_sets = carry
            new_sets = []
            for label_set, piece, slope_set in zip(label_sets, pieces, slope_sets):
                cosine = lax.dot_general(
                    piece, unit_rows, (((1,), (1,)), ((), ())), preferred_element_type=jnp.float32
                )
                positive = label_set[:, None] == class_ids[None, :]
                dlogit = logit_grad(cosine, positive)
                grad_unit = grad_unit + lax.dot_general(
                    dlogit, piece, (((0,), (0,)), ((), ())), preferred_element_type=jnp.float32
                )
                new_sets.append(dlogit)
            return (grad_unit, tuple(new_sets))

        return folder

    empty_grad = jnp.zeros((cls_rows, width), jnp.float32)
    empty_slope = jnp.zeros((total_rows, cls_rows), jnp.bfloat16)
    face_sets = tuple((faces[batch_number] for batch_number in range(batches)))
    label_sets = tuple((labels[batch_number] for batch_number in range(batches)))
    empty_sets = tuple((empty_slope for batch_number in range(batches)))
    grad_unit, slope_sets = fold_faces(face_sets, make_fold(label_sets), (empty_grad, empty_sets))

    def term(start, count):
        return jnp.concatenate(
            [
                jnp.dot(slope_set, unit_rows, preferred_element_type=jnp.float32)
                for slope_set in slope_sets
            ],
            axis=1,
        )

    joined = spread_back(term, face_rows)
    face_grad = joined.reshape(face_rows, batches, width).transpose(1, 0, 2)
    new_centres, new_momentum = update(master, length, unit_wide, grad_unit, momentum)
    return (face_grad, new_centres, new_momentum)


def solution(mesh):
    in_specs = (P(None, ("dp", "cls"), None), P(), P(("dp", "cls"), None), P(("dp", "cls"), None))
    out_specs = (P(None, ("dp", "cls"), None), P(("dp", "cls"), None), P(("dp", "cls"), None))
    return jax.shard_map(local, mesh=mesh, in_specs=in_specs, out_specs=out_specs, check_vma=False)
```

profile of v0, /device:TPU:0, one launch (start us, length us, event | category | flops | bytes accessed | tf_op | source)
XLA Modules:
  0.0 139.6 jit_solution(18151039587848830202)
XLA Ops:
  7.2 0.0 reduce-scatter.2.cloned.1.call-start
  7.2 0.0 copy-start.2
  7.2 0.7 copy-done.2
  7.9 0.0 copy-start.1
  7.9 0.7 copy-done.1
  8.6 27.9 %all-gather = bf16[8,1,512]{2,1,0:T(2,128)(2,1)S(1)} all-gather(bf16[1,1,512]{2,1,0:T(2,128)(2,1)S(1)} %get-tuple-element.14), channel_id=2, replica_groups=mesh['dp'=4,'cls'=8] {'cls'}, dimensions={0}, use_global_device_ids=true | all-gather | bytes 9216 | tf_op jit(solution)/shard_map/all_gather | solution.py:49
  36.5 26.1 %all-gather.2 = bf16[8,1,512]{2,1,0:T(2,128)(2,1)S(1)} all-gather(bf16[1,1,512]{2,1,0:T(2,128)(2,1)S(1)} %get-tuple-element.15), channel_id=4, replica_groups=mesh['dp'=4,'cls'=8] {'cls'}, dimensions={0}, use_global_device_ids=true | all-gather | bytes 9216 | tf_op jit(solution)/shard_map/all_gather | solution.py:49
  62.6 5.2 %all-gather.3 = bf16[32,1,512]{2,0,1:T(8,128)(2,1)S(1)} all-gather(bf16[8,1,512]{2,0,1:T(8,128)(2,1)S(1)} %copy.23), channel_id=5, replica_groups=mesh['dp'=4,'cls'=8] {'dp'}, dimensions={0}, use_global_device_ids=true | all-gather | bytes 40960 | tf_op jit(solution)/shard_map/all_gather | solution.py:54
  67.8 5.2 %all-gather.1 = bf16[32,1,512]{2,0,1:T(8,128)(2,1)S(1)} all-gather(bf16[8,1,512]{2,0,1:T(8,128)(2,1)S(1)} %copy.21), channel_id=3, replica_groups=mesh['dp'=4,'cls'=8] {'dp'}, dimensions={0}, use_global_device_ids=true | all-gather | bytes 40960 | tf_op jit(solution)/shard_map/all_gather | solution.py:54
  73.0 1.3 copy.19
  74.2 0.2 fusion.2
  74.4 0.1 fusion.5
  74.5 0.3 fusion.9
  74.8 0.2 convolution_convert_fusion
  75.0 0.3 fusion.7
  75.3 0.2 convolution_convert_fusion.1
  75.5 0.6 pad_maximum_fusion
  76.2 0.0 reduce-scatter.2.cloned.1.call-update
  76.2 0.0 copy-start
  76.2 0.3 fusion.12
  76.6 0.7 copy-done
  77.2 0.2 copy.24
  77.5 0.4 multiply_reduce_fusion
  77.9 0.4 fusion.15
  78.2 0.2 fusion.4
  78.5 1.0 copy.27
  79.5 1.0 copy.26
  80.5 0.0 copy-start.3
  80.5 0.7 copy-done.3
  81.1 0.6 dynamic-slice
  81.7 12.1 %reduce-scatter.2.cloned.1.call-done = bf16[8,1024]{1,0:T(8,128)(2,1)} async-done(((bf16[32,1024]{1,0:T(8,128)(2,1)}), bf16[8,1024]{1,0:T(8,128)(2,1)}) %reduce-scatter.2.cloned.1.call-update) | async-done | bytes 16400 | tf_op jit(solution)/shard_map/reduce_scatter | solution.py:60
  93.8 37.8 %all-reduce = f32[8,1024]{1,0:T(8,128)S(1)} all-reduce(bf16[8,1024]{1,0:T(8,128)(2,1)} %reduce-scatter.2.cloned.1.call-done), channel_id=7, replica_groups=mesh['dp'=4,'cls'=8] {'cls'}, use_global_device_ids=true, to_apply=%region_2.3.clone | all-reduce | flops 8192 | bytes 49152
  131.6 1.2 constant_dynamic-slice_fusion
  (6 shorter events, 0.0 us)
Async XLA Ops:
  7.2 86.6 %reduce-scatter.2.cloned.1.call-start = ((), (), s32[]{:S(2)}) async-start(), calls=%async_computation.1 | async-start | bytes 81920 | tf_op jit(solution)/shard_map/reduce_scatter | solution.py:60
  7.2 0.7 copy-start.2
  7.9 0.7 copy-start.1
  76.2 1.0 copy-start
  80.5 0.7 copy-start.3
Sparse Core Ops, SparseCore 0:
  76.3 17.4 reduce-scatter.1
where the time goes:
time: 140 us
  blocking collectives  102 us (73%)
  between operations  14.1 us (10%)
  waiting for transfers between devices  12.1 us (9%)
  local copies, waits for them, and re-layouts  7.99 us (6%)
  matrix products  1.74 us (1%)
  other arithmetic  1.51 us (1%)
    all_gather x2, blocking collectives, fold_faces(): lax.all_gather(as_sent(pieces), 'cls', axis=0, tiled=True)  54 us
    unnamed x1, blocking collectives  37.8 us
    reduce_scatter x1, waiting for transfers between devices, spread_back(): lax.psum_scatter(term(jnp.int32(0), face_rows * lax.axis_size('cls') * la...  12.1 us
    all_gather x2, blocking collectives, fold_faces(): lax.all_gather(part, 'dp', axis=0, tiled=True)  10.3 us
    unnamed x15, local copies, waits for them, and re-layouts  7.98 us
  transfers between devices with their start and end apart: 1, of which 1 were waited for; matrix products, arithmetic and copies ran while one was open for 3% of the time, Pallas kernels for 0%

commit v1 on v0

v1 whole, which is shorter than its diff:
```python
import functools
import jax
import jax.numpy as jnp
from jax import lax
from jax.experimental import pallas as pl
from jax.experimental.pallas import tpu as pltpu
from jax.sharding import PartitionSpec as P

SCALE = 30.0
MARGIN = 0.4
POS_WEIGHT = 0.7
BIAS = 6.5
EPS = 1e-06
MOMENTUM_RATE = 0.9
LEARN_RATE = 0.1
DECAY = 0.0005
MESH = pl.DeviceIdType.MESH


def logit_grad(cosine, positive):
    halfway = (cosine + 1.0) * 0.5
    square = halfway * halfway
    shaped = 2.0 * square * halfway - 1.0
    slopes = 3.0 * square
    argument = jnp.where(
        positive, -(SCALE * (shaped - MARGIN) + BIAS), SCALE * (shaped + MARGIN) + BIAS
    )
    weight = jnp.where(positive, -POS_WEIGHT * SCALE, (1.0 - POS_WEIGHT) * SCALE)
    return (weight * jax.nn.sigmoid(argument) * slopes).astype(jnp.bfloat16)


def kernel(
    devices, group, face_rows, chunk, block,
    faces_hbm, labels_hbm, centres_hbm, momentum_hbm,
    face_grad, new_centres_hbm, new_momentum_hbm,
    raw, own, gathered, labels, centres, momentum, unit, inverse, grad, outgoing, incoming,
    new_centres, new_momentum,
    local_sems, gather_send, gather_recv, scatter_send, scatter_recv,
):
    outer, inner = lax.axis_index("dp"), lax.axis_index("cls")
    me = outer * group + inner
    rows, width = centres.shape
    batches = raw.shape[0]
    slot_rows = batches * face_rows

    def device(index):
        return (index // group, index % group)

    load_faces = pltpu.make_async_copy(faces_hbm, raw, local_sems.at[0])
    load_labels = pltpu.make_async_copy(labels_hbm, labels, local_sems.at[1])
    load_centres = pltpu.make_async_copy(centres_hbm, centres, local_sems.at[2])
    load_momentum = pltpu.make_async_copy(momentum_hbm, momentum, local_sems.at[3])
    load_faces.start()
    load_centres.start()
    load_labels.start()
    load_momentum.start()

    barrier = pltpu.get_barrier_semaphore()

    def greet(step, carry):
        peer = lax.rem(me + step, devices)
        pl.semaphore_signal(barrier, inc=1, device_id=device(peer), device_id_type=MESH)
        return carry

    lax.fori_loop(1, devices, greet, 0)
    load_faces.wait()
    own[...] = raw[...].reshape(slot_rows, width)
    pl.semaphore_wait(barrier, devices - 1)

    def gather(step, carry):
        peer = lax.rem(me + step, devices)
        pltpu.make_async_remote_copy(
            src_ref=own, dst_ref=gathered.at[me], send_sem=gather_send, recv_sem=gather_recv,
            device_id=device(peer), device_id_type=MESH,
        ).start()
        return carry

    lax.fori_loop(1, devices, gather, 0)
    pltpu.make_async_copy(own, gathered.at[me], gather_recv).start()

    load_centres.wait()

    def normalize(step, carry):
        part = pl.ds(pl.multiple_of(step * block, block), block)
        master = centres[part, :].astype(jnp.float32)
        scale = lax.rsqrt(jnp.sum(master * master, axis=1, keepdims=True) + EPS)
        inverse[part, :] = scale
        unit[part, :] = (master * scale).astype(jnp.bfloat16)
        return carry

    lax.fori_loop(0, rows // block, normalize, 0)
    load_labels.wait()
    count = chunk * slot_rows
    class_ids = me * rows + lax.broadcasted_iota(jnp.int32, (count, rows), 1)

    def label_column(first):
        shape = (count, labels.shape[1])
        row = lax.broadcasted_iota(jnp.int32, shape, 0)
        lane = lax.broadcasted_iota(jnp.int32, shape, 1)
        inside = row % slot_rows
        wanted = (first + row // slot_rows) * face_rows + inside % face_rows
        batch = inside // face_rows
        values = jnp.zeros(shape, jnp.float32)
        for number in range(batches):
            line = labels[number : number + 1, :].astype(jnp.float32)
            values = jnp.where((lane == wanted) & (batch == number), line, values)
        return jnp.sum(values, axis=1, keepdims=True).astype(jnp.int32)

    chunks = devices // chunk
    if chunks == 1:
        column = label_column(0)
    pltpu.make_async_copy(gathered, gathered, gather_recv).wait()

    def fold(step):
        if chunks == 1:
            slots = slice(None)
            target = column
        else:
            slots = pl.ds(step * chunk, chunk)
            target = label_column(step * chunk)
        piece = gathered[slots].reshape(count, width)
        cosine = lax.dot_general(
            piece, unit[...], (((1,), (1,)), ((), ())), preferred_element_type=jnp.float32
        )
        dlogit = logit_grad(cosine, target == class_ids)
        term = jnp.dot(dlogit, unit[...], preferred_element_type=jnp.float32)
        outgoing[slots] = term.astype(jnp.bfloat16).reshape(chunk, slot_rows, width)
        return dlogit, piece

    def outer_product(dlogit, piece):
        return lax.dot_general(
            dlogit, piece, (((0,), (0,)), ((), ())), preferred_element_type=jnp.float32
        )

    def scatter(step, carry):
        peer = lax.rem(me + step, devices)
        pltpu.make_async_remote_copy(
            src_ref=outgoing.at[peer], dst_ref=incoming.at[me],
            send_sem=scatter_send, recv_sem=scatter_recv,
            device_id=device(peer), device_id_type=MESH,
        ).start()
        return carry

    if chunks == 1:
        dlogit, piece = fold(0)
        lax.fori_loop(1, devices, scatter, 0)
        pltpu.make_async_copy(outgoing.at[me], incoming.at[me], scatter_recv).start()
        grad[...] = outer_product(dlogit, piece)
    else:
        grad[...] = jnp.zeros_like(grad)

        def step_chunk(step, carry):
            dlogit, piece = fold(step)
            grad[...] += outer_product(dlogit, piece)
            return carry

        lax.fori_loop(0, chunks, step_chunk, 0)
        lax.fori_loop(1, devices, scatter, 0)
        pltpu.make_async_copy(outgoing.at[me], incoming.at[me], scatter_recv).start()

    load_momentum.wait()

    def update(step, carry):
        part = pl.ds(pl.multiple_of(step * block, block), block)
        master = centres[part, :].astype(jnp.float32)
        scale = inverse[part, :]
        wide = master * scale
        grad_unit = grad[part, :]
        radial = jnp.sum(wide * grad_unit, axis=1, keepdims=True)
        grad_centre = (grad_unit - wide * radial) * scale
        velocity = (
            MOMENTUM_RATE * momentum[part, :].astype(jnp.float32) + grad_centre + DECAY * master
        )
        new_centres[part, :] = (master - LEARN_RATE * velocity).astype(jnp.bfloat16)
        new_momentum[part, :] = velocity.astype(jnp.bfloat16)
        return carry

    lax.fori_loop(0, rows // block, update, 0)
    store_centres = pltpu.make_async_copy(new_centres, new_centres_hbm, local_sems.at[4])
    store_momentum = pltpu.make_async_copy(new_momentum, new_momentum_hbm, local_sems.at[5])
    store_centres.start()
    store_momentum.start()

    pltpu.make_async_copy(incoming, incoming, scatter_recv).wait()
    if chunks == 1:
        total = jnp.sum(incoming[...].astype(jnp.float32), axis=0)
    else:
        total = lax.fori_loop(
            0, chunks,
            lambda step, sofar: sofar
            + jnp.sum(incoming[pl.ds(step * chunk, chunk)].astype(jnp.float32), axis=0),
            jnp.zeros((slot_rows, width), jnp.float32),
        )
    face_grad[...] = total.reshape(batches, face_rows, width)

    if devices > 1:
        others = gathered.at[pl.ds(0, devices - 1)]
        pltpu.make_async_copy(others, others, gather_send).wait()
        others = outgoing.at[pl.ds(0, devices - 1)]
        pltpu.make_async_copy(others, others, scatter_send).wait()
    store_centres.wait()
    store_momentum.wait()


def local(devices, group, faces, labels, centres, momentum):
    batches, face_rows, width = faces.shape
    rows = centres.shape[0]
    slot_rows = batches * face_rows
    chunk = devices
    while chunk * slot_rows > 64 and chunk % 2 == 0:
        chunk //= 2
    block = 64 if rows % 64 == 0 else rows
    half = jnp.bfloat16
    hbm = pl.BlockSpec(memory_space=pltpu.HBM)
    slots = pltpu.VMEM((devices, slot_rows, width), half)
    square = pltpu.VMEM((rows, width), half)
    return pl.pallas_call(
        functools.partial(kernel, devices, group, face_rows, chunk, block),
        out_shape=(
            jax.ShapeDtypeStruct(faces.shape, jnp.float32),
            jax.ShapeDtypeStruct(centres.shape, half),
            jax.ShapeDtypeStruct(momentum.shape, half),
        ),
        in_specs=[hbm] * 4,
        out_specs=(pl.BlockSpec(memory_space=pltpu.VMEM), hbm, hbm),
        scratch_shapes=[
            pltpu.VMEM(faces.shape, half),
            pltpu.VMEM((slot_rows, width), half),
            slots,
            pltpu.VMEM(labels.shape, jnp.int32),
            square, square, square,
            pltpu.VMEM((rows, 1), jnp.float32),
            pltpu.VMEM((rows, width), jnp.float32),
            slots, slots,
            square, square,
            pltpu.SemaphoreType.DMA((6,)),
            pltpu.SemaphoreType.DMA,
            pltpu.SemaphoreType.DMA,
            pltpu.SemaphoreType.DMA,
            pltpu.SemaphoreType.DMA,
        ],
        compiler_params=pltpu.CompilerParams(collective_id=0, has_side_effects=True),
    )(faces, labels, centres, momentum)


def solution(mesh):
    group = mesh.shape["cls"]
    devices = mesh.shape["dp"] * group
    in_specs = (P(None, ("dp", "cls"), None), P(), P(("dp", "cls"), None), P(("dp", "cls"), None))
    out_specs = (P(None, ("dp", "cls"), None), P(("dp", "cls"), None), P(("dp", "cls"), None))
    return jax.shard_map(
        functools.partial(local, devices, group),
        mesh=mesh, in_specs=in_specs, out_specs=out_specs, check_vma=False,
    )
```

time: 140 us -> 23.8 us (0.17)
  blocking collectives: 102 us -> 0 us
  Pallas kernels: 0 us -> 17.7 us
  between operations: 14.1 us -> 0.65 us
  waiting for transfers between devices: 12.1 us -> 0 us
  local copies, waits for them, and re-layouts: 7.99 us -> 5.27 us
  matrix products: 1.74 us -> 0 us
  other arithmetic: 1.51 us -> 0 us
    all_gather x4 -> x0, blocking collectives: 64.4 us -> none  [the longest x2 54 us: fold_faces(): lax.all_gather(as_sent(pieces), 'cls', axis=0, tiled=True)]
    unnamed x1 -> x0, blocking collectives: 37.8 us -> none
    pallas_call x0 -> x1, Pallas kernels: none -> 17.7 us  [local(): pl.pallas_call(functools.partial(kernel, devices, group, face_rows, chunk...]
    reduce_scatter x1 -> x0, waiting for transfers between devices: 12.1 us -> none  [spread_back(): lax.psum_scatter(term(jnp.int32(0), face_rows * lax.axis_size('cls') * la...]
    unnamed x15 -> x8, local copies, waits for them, and re-layouts: 7.98 us -> 5.27 us
    dot_general x6 -> x0, matrix products: 1.74 us -> none  [the longest x2 0.73 us: folder(): lax.dot_general(dlogit, piece, (((0,), (0,)), ((), ())), preferred_elemen...]
  transfers between devices with their start and end apart: 1 -> 0, of which waited for: 1 -> 0; matrix products, arithmetic and copies ran while one was open for 3% -> 0% of each run, Pallas kernels for 0% -> 0%
where the time goes in v1:
time: 23.8 us; the launch traced here: 23.6 us
  Pallas kernels  17.7 us (74%)
  local copies, waits for them, and re-layouts  5.27 us (22%)
  between operations  0.65 us (3%)
    pallas_call x1, Pallas kernels, local(): pl.pallas_call(functools.partial(kernel, devices, group, face_rows, chunk...  17.7 us
    unnamed x8, local copies, waits for them, and re-layouts  5.27 us

profile of v1, /device:TPU:0, one launch (start us, length us, event | category | flops | bytes accessed | tf_op | source)
XLA Modules:
  0.0 23.6 jit_solution(2150649196103315234)
XLA Ops:
  0.6 1.3 %copy.7.faces_hbm = bf16[2,1,512]{2,1,0:T(2,128)(2,1)} copy(bf16[2,1,512]{2,0,1:T(2,128)(2,1)} %param.4) | data formatting | bytes 4096 | tf_op args[0]
  1.9 17.7 %shard_map.67 = (f32[2,1,512]{2,1,0:T(1,128)}, bf16[512,512]{1,0:T(8,128)(2,1)}, bf16[512,512]{1,0:T(8,128)(2,1)}) custom-call(bf16[2,1,512]{2,1,0:T(2,128)(2,1)} %copy.7.faces_hbm, s32[2,32]{1,0:T(2,128)} %labels_hbm.1, bf16[512,512]{1,0:T(8,128)(2,1)} %centres_hbm.1, bf16[512,512]{1,0:T(8,128)(2,1)} %momentum_hbm.1), custom_call_target="tpu_custom_call" | custom-call | tf_op jit(solution)/shard_map/pallas_call | solution.py:217
  19.6 0.0 copy-start.1
  19.6 0.7 %copy-done.1 = f32[2,1,512]{2,1,0:T(1,128)S(1)} copy-done((f32[2,1,512]{2,1,0:T(1,128)S(1)}, f32[2,1,512]{2,1,0:T(1,128)}, u32[]{:S(2)}) %copy-start.1) | copy-done | bytes 4120
  20.3 0.6 %copy.11 = f32[2,1,512]{2,1,0:T(1,128)} copy(f32[2,1,512]{2,1,0:T(1,128)S(1)} %copy-done.1) | data formatting | bytes 8192
  20.8 0.0 copy-start
  20.8 1.9 %copy.12 = bf16[512,512]{1,0:T(8,128)(2,1)} copy(bf16[512,512]{1,0:T(8,128)(2,1)} %get-tuple-element.7) | data formatting | bytes 1048576
  22.8 0.0 copy-done
  22.8 0.8 %copy.13 = bf16[512,512]{1,0:T(8,128)(2,1)} copy(bf16[512,512]{1,0:T(8,128)(2,1)S(1)} %copy-done) | data formatting | bytes 1048576
Async XLA Ops:
  19.6 0.7 %copy-start.1 = (f32[2,1,512]{2,1,0:T(1,128)S(1)}, f32[2,1,512]{2,1,0:T(1,128)}, u32[]{:S(2)}) copy-start(f32[2,1,512]{2,1,0:T(1,128)} %get-tuple-element.6) | copy-start | bytes 12292
  20.8 1.9 %copy-start = (bf16[512,512]{1,0:T(8,128)(2,1)S(1)}, bf16[512,512]{1,0:T(8,128)(2,1)}, u32[]{:S(2)}) copy-start(bf16[512,512]{1,0:T(8,128)(2,1)} %get-tuple-element.8) | copy-start | bytes 1572868

commit v2 on v1

--- a/solution.py
+++ b/solution.py
@@ -32,21 +32,20 @@
 def kernel(
     devices, group, face_rows, chunk, block,
     faces_hbm, labels_hbm, centres_hbm, momentum_hbm,
-    face_grad, new_centres_hbm, new_momentum_hbm,
-    raw, own, gathered, labels, centres, momentum, unit, inverse, grad, outgoing, incoming,
-    new_centres, new_momentum,
+    face_grad, new_centres, new_momentum,
+    own, gathered, labels, centres, momentum, unit, inverse, grad, outgoing, incoming,
     local_sems, gather_send, gather_recv, scatter_send, scatter_recv,
 ):
     outer, inner = lax.axis_index("dp"), lax.axis_index("cls")
     me = outer * group + inner
     rows, width = centres.shape
-    batches = raw.shape[0]
+    batches = labels.shape[0]
     slot_rows = batches * face_rows
 
     def device(index):
         return (index // group, index % group)
 
-    load_faces = pltpu.make_async_copy(faces_hbm, raw, local_sems.at[0])
+    load_faces = pltpu.make_async_copy(faces_hbm, own, local_sems.at[0])
     load_labels = pltpu.make_async_copy(labels_hbm, labels, local_sems.at[1])
     load_centres = pltpu.make_async_copy(centres_hbm, centres, local_sems.at[2])
     load_momentum = pltpu.make_async_copy(momentum_hbm, momentum, local_sems.at[3])
@@ -64,7 +63,6 @@
 
     lax.fori_loop(1, devices, greet, 0)
     load_faces.wait()
-    own[...] = raw[...].reshape(slot_rows, width)
     pl.semaphore_wait(barrier, devices - 1)
 
     def gather(step, carry):
@@ -97,9 +95,8 @@
         shape = (count, labels.shape[1])
         row = lax.broadcasted_iota(jnp.int32, shape, 0)
         lane = lax.broadcasted_iota(jnp.int32, shape, 1)
-        inside = row % slot_rows
-        wanted = (first + row // slot_rows) * face_rows + inside % face_rows
-        batch = inside // face_rows
+        wanted = first * face_rows + row // batches
+        batch = row % batches
         values = jnp.zeros(shape, jnp.float32)
         for number in range(batches):
             line = labels[number : number + 1, :].astype(jnp.float32)
@@ -176,11 +173,6 @@
         return carry
 
     lax.fori_loop(0, rows // block, update, 0)
-    store_centres = pltpu.make_async_copy(new_centres, new_centres_hbm, local_sems.at[4])
-    store_momentum = pltpu.make_async_copy(new_momentum, new_momentum_hbm, local_sems.at[5])
-    store_centres.start()
-    store_momentum.start()
-
     pltpu.make_async_copy(incoming, incoming, scatter_recv).wait()
     if chunks == 1:
         total = jnp.sum(incoming[...].astype(jnp.float32), axis=0)
@@ -191,15 +183,15 @@
             + jnp.sum(incoming[pl.ds(step * chunk, chunk)].astype(jnp.float32), axis=0),
             jnp.zeros((slot_rows, width), jnp.float32),
         )
-    face_grad[...] = total.reshape(batches, face_rows, width)
+    total = total.reshape(face_rows, batches, width)
+    for batch in range(batches):
+        face_grad[batch] = total[:, batch, :]
 
     if devices > 1:
         others = gathered.at[pl.ds(0, devices - 1)]
         pltpu.make_async_copy(others, others, gather_send).wait()
         others = outgoing.at[pl.ds(0, devices - 1)]
         pltpu.make_async_copy(others, others, scatter_send).wait()
-    store_centres.wait()
-    store_momentum.wait()
 
 
 def local(devices, group, faces, labels, centres, momentum):
@@ -212,19 +204,19 @@
     block = 64 if rows % 64 == 0 else rows
     half = jnp.bfloat16
     hbm = pl.BlockSpec(memory_space=pltpu.HBM)
+    vmem = pl.BlockSpec(memory_space=pltpu.VMEM)
     slots = pltpu.VMEM((devices, slot_rows, width), half)
     square = pltpu.VMEM((rows, width), half)
     return pl.pallas_call(
         functools.partial(kernel, devices, group, face_rows, chunk, block),
         out_shape=(
-            jax.ShapeDtypeStruct(faces.shape, jnp.float32),
-            jax.ShapeDtypeStruct(centres.shape, half),
-            jax.ShapeDtypeStruct(momentum.shape, half),
+            pltpu.VMEM(faces.shape, jnp.float32),
+            pltpu.VMEM(centres.shape, half),
+            pltpu.VMEM(momentum.shape, half),
         ),
         in_specs=[hbm] * 4,
-        out_specs=(pl.BlockSpec(memory_space=pltpu.VMEM), hbm, hbm),
+        out_specs=(vmem, vmem, vmem),
         scratch_shapes=[
-            pltpu.VMEM(faces.shape, half),
             pltpu.VMEM((slot_rows, width), half),
             slots,
             pltpu.VMEM(labels.shape, jnp.int32),
@@ -232,15 +224,14 @@
             pltpu.VMEM((rows, 1), jnp.float32),
             pltpu.VMEM((rows, width), jnp.float32),
             slots, slots,
-            square, square,
-            pltpu.SemaphoreType.DMA((6,)),
+            pltpu.SemaphoreType.DMA((4,)),
             pltpu.SemaphoreType.DMA,
             pltpu.SemaphoreType.DMA,
             pltpu.SemaphoreType.DMA,
             pltpu.SemaphoreType.DMA,
         ],
         compiler_params=pltpu.CompilerParams(collective_id=0, has_side_effects=True),
-    )(faces, labels, centres, momentum)
+    )(faces.transpose(1, 0, 2).reshape(slot_rows, width), labels, centres, momentum)
 
 
 def solution(mesh):

time: 23.8 us -> 20.2 us (0.85)
  local copies, waits for them, and re-layouts: 5.27 us -> 2.18 us
  Pallas kernels: 17.7 us -> 17.3 us
    unnamed x8 -> x3, local copies, waits for them, and re-layouts: 5.27 us -> 2.18 us
    pallas_call x1, Pallas kernels: 17.7 us -> 17.3 us  [local(): pl.pallas_call(functools.partial(kernel, devices, group, face_rows, chunk...]
where the time goes in v2:
time: 20.2 us; the launch traced here: 20.1 us
  Pallas kernels  17.3 us (86%)
  local copies, waits for them, and re-layouts  2.18 us (11%)
  between operations  0.64 us (3%)
    pallas_call x1, Pallas kernels, local(): pl.pallas_call(functools.partial(kernel, devices, group, face_rows, chunk...  17.3 us
    unnamed x3, local copies, waits for them, and re-layouts  2.18 us

profile of v2, /device:TPU:0, one launch (start us, length us, event | category | flops | bytes accessed | tf_op | source)
XLA Modules:
  0.0 20.1 jit_solution(10685427084502452832)
XLA Ops:
  0.6 17.3 %shard_map.67 = (f32[2,1,512]{2,1,0:T(1,128)S(1)}, bf16[512,512]{1,0:T(8,128)(2,1)S(1)}, bf16[512,512]{1,0:T(8,128)(2,1)S(1)}) custom-call(bf16[2,512]{1,0:T(2,128)(2,1)} %bitcast.1, s32[2,32]{1,0:T(2,128)} %labels_hbm.1, bf16[512,512]{1,0:T(8,128)(2,1)} %centres_hbm.1, bf16[512,512]{1,0:T(8,128)(2,1)} %momentum_hbm.1), custom_call_target="tpu_custom_call" | custom-call | tf_op jit(solution)/shard_map/pallas_call | solution.py:210
  17.9 0.6 %copy.10 = f32[2,1,512]{2,1,0:T(1,128)} copy(f32[2,1,512]{2,1,0:T(1,128)S(1)} %get-tuple-element.3) | data formatting | bytes 8192
  18.5 0.8 %copy.11 = bf16[512,512]{1,0:T(8,128)(2,1)} copy(bf16[512,512]{1,0:T(8,128)(2,1)S(1)} %get-tuple-element.4) | data formatting | bytes 1048576
  19.3 0.8 %copy.12 = bf16[512,512]{1,0:T(8,128)(2,1)} copy(bf16[512,512]{1,0:T(8,128)(2,1)S(1)} %get-tuple-element.5) | data formatting | bytes 1048576

commit v3 on v2

--- a/solution.py
+++ b/solution.py
@@ -192,6 +192,19 @@
         pltpu.make_async_copy(others, others, gather_send).wait()
         others = outgoing.at[pl.ds(0, devices - 1)]
         pltpu.make_async_copy(others, others, scatter_send).wait()
+
+
+def store_kernel(*refs):
+    count = (len(refs) - 1) // 2
+    sems = refs[-1]
+    stores = [
+        pltpu.make_async_copy(refs[number], refs[count + number], sems.at[number])
+        for number in range(count)
+    ]
+    for store in stores:
+        store.start()
+    for store in stores:
+        store.wait()
 
 
 def local(devices, group, faces, labels, centres, momentum):
@@ -207,7 +220,7 @@
     vmem = pl.BlockSpec(memory_space=pltpu.VMEM)
     slots = pltpu.VMEM((devices, slot_rows, width), half)
     square = pltpu.VMEM((rows, width), half)
-    return pl.pallas_call(
+    results = pl.pallas_call(
         functools.partial(kernel, devices, group, face_rows, chunk, block),
         out_shape=(
             pltpu.VMEM(faces.shape, jnp.float32),
@@ -232,6 +245,14 @@
         ],
         compiler_params=pltpu.CompilerParams(collective_id=0, has_side_effects=True),
     )(faces.transpose(1, 0, 2).reshape(slot_rows, width), labels, centres, momentum)
+    anywhere = pl.BlockSpec(memory_space=pl.ANY)
+    return pl.pallas_call(
+        store_kernel,
+        out_shape=tuple(jax.ShapeDtypeStruct(part.shape, part.dtype) for part in results),
+        in_specs=[anywhere] * len(results),
+        out_specs=(hbm,) * len(results),
+        scratch_shapes=[pltpu.SemaphoreType.DMA((len(results),))],
+    )(*(pltpu.with_memory_space_constraint(part, pltpu.VMEM) for part in results))
 
 
 def solution(mesh):

time: 20.2 us -> 19.1 us (0.946)
  local copies, waits for them, and re-layouts: 2.18 us -> 0 us
  Pallas kernels: 17.3 us -> 18.3 us
    unnamed x3 -> x0, local copies, waits for them, and re-layouts: 2.18 us -> none
    pallas_call x0 -> x1, Pallas kernels: none -> 1 us  [local(): pl.pallas_call(store_kernel, out_shape=tuple((jax.ShapeDtypeStruct(part.s...]
where the time goes in v3:
time: 19.1 us; the launch traced here: 18.9 us
  Pallas kernels  18.3 us (96%)
  between operations  0.64 us (3%)
    pallas_call x1, Pallas kernels, local(): pl.pallas_call(functools.partial(kernel, devices, group, face_rows, chunk...  17.3 us
    pallas_call x1, Pallas kernels, local(): pl.pallas_call(store_kernel, out_shape=tuple((jax.ShapeDtypeStruct(part.s...  1 us

profile of v3, /device:TPU:0, one launch (start us, length us, event | category | flops | bytes accessed | tf_op | source)
XLA Modules:
  0.0 18.9 jit_solution(12407275114898875695)
XLA Ops:
  0.6 17.3 %shard_map.67 = (f32[2,1,512]{2,1,0:T(1,128)S(1)}, bf16[512,512]{1,0:T(8,128)(2,1)S(1)}, bf16[512,512]{1,0:T(8,128)(2,1)S(1)}) custom-call(bf16[2,512]{1,0:T(2,128)(2,1)} %bitcast.1, s32[2,32]{1,0:T(2,128)} %labels_hbm.1, bf16[512,512]{1,0:T(8,128)(2,1)} %centres_hbm.1, bf16[512,512]{1,0:T(8,128)(2,1)} %momentum_hbm.1), custom_call_target="tpu_custom_call" | custom-call | tf_op jit(solution)/shard_map/pallas_call | solution.py:223
  17.9 1.0 %shard_map.68 = (f32[2,1,512]{2,1,0:T(1,128)}, bf16[512,512]{1,0:T(8,128)(2,1)}, bf16[512,512]{1,0:T(8,128)(2,1)}) custom-call(f32[2,1,512]{2,1,0:T(1,128)S(1)} %get-tuple-element.6.refs_0_, bf16[512,512]{1,0:T(8,128)(2,1)S(1)} %get-tuple-element.7.refs_1_, bf16[512,512]{1,0:T(8,128)(2,1)S(1)} %get-tuple-element.8.refs_2_), custom_call_target="tpu_custom_call" | custom-call | tf_op jit(solution)/shard_map/pallas_call | solution.py:249

commit v4 on v3

--- a/solution.py
+++ b/solution.py
@@ -42,8 +42,18 @@
     batches = labels.shape[0]
     slot_rows = batches * face_rows
 
+    across = devices // group
+    place = inner * across + outer
+
     def device(index):
         return (index // group, index % group)
+
+    def early(step):
+        spot = jnp.where(step >= place, step + 1, step)
+        return (spot % across) * group + spot // across
+
+    def late(step):
+        return early(devices - 2 - step)
 
     load_faces = pltpu.make_async_copy(faces_hbm, own, local_sems.at[0])
     load_labels = pltpu.make_async_copy(labels_hbm, labels, local_sems.at[1])
@@ -61,19 +71,19 @@
         pl.semaphore_signal(barrier, inc=1, device_id=device(peer), device_id_type=MESH)
         return carry
 
-    lax.fori_loop(1, devices, greet, 0)
+    lax.fori_loop(1, devices, greet, 0, unroll=devices <= 64)
     load_faces.wait()
     pl.semaphore_wait(barrier, devices - 1)
 
     def gather(step, carry):
-        peer = lax.rem(me + step, devices)
+        peer = late(step)
         pltpu.make_async_remote_copy(
             src_ref=own, dst_ref=gathered.at[me], send_sem=gather_send, recv_sem=gather_recv,
             device_id=device(peer), device_id_type=MESH,
         ).start()
         return carry
 
-    lax.fori_loop(1, devices, gather, 0)
+    lax.fori_loop(0, devices - 1, gather, 0, unroll=devices <= 64)
     pltpu.make_async_copy(own, gathered.at[me], gather_recv).start()
 
     load_centres.wait()
@@ -130,7 +140,7 @@
         )
 
     def scatter(step, carry):
-        peer = lax.rem(me + step, devices)
+        peer = early(step)
         pltpu.make_async_remote_copy(
             src_ref=outgoing.at[peer], dst_ref=incoming.at[me],
             send_sem=scatter_send, recv_sem=scatter_recv,
@@ -140,7 +150,7 @@
 
     if chunks == 1:
         dlogit, piece = fold(0)
-        lax.fori_loop(1, devices, scatter, 0)
+        lax.fori_loop(0, devices - 1, scatter, 0, unroll=devices <= 64)
         pltpu.make_async_copy(outgoing.at[me], incoming.at[me], scatter_recv).start()
         grad[...] = outer_product(dlogit, piece)
     else:
@@ -152,7 +162,7 @@
             return carry
 
         lax.fori_loop(0, chunks, step_chunk, 0)
-        lax.fori_loop(1, devices, scatter, 0)
+        lax.fori_loop(0, devices - 1, scatter, 0)
         pltpu.make_async_copy(outgoing.at[me], incoming.at[me], scatter_recv).start()
 
     load_momentum.wait()

time: 19.1 us -> 18.4 us (0.963)
  Pallas kernels: 18.3 us -> 17.6 us
    pallas_call x1, Pallas kernels: 17.3 us -> 16.6 us  [local(): pl.pallas_call(functools.partial(kernel, devices, group, face_rows, chunk...]
where the time goes in v4:
time: 18.4 us; the launch traced here: 18.2 us
  Pallas kernels  17.6 us (96%)
  between operations  0.64 us (3%)
    pallas_call x1, Pallas kernels, local(): pl.pallas_call(functools.partial(kernel, devices, group, face_rows, chunk...  16.6 us
    pallas_call x1, Pallas kernels, local(): pl.pallas_call(store_kernel, out_shape=tuple((jax.ShapeDtypeStruct(part.s...  1 us

profile of v4, /device:TPU:0, one launch (start us, length us, event | category | flops | bytes accessed | tf_op | source)
XLA Modules:
  0.0 18.2 jit_solution(8960012531004458225)
XLA Ops:
  0.6 16.6 %shard_map.67 = (f32[2,1,512]{2,1,0:T(1,128)S(1)}, bf16[512,512]{1,0:T(8,128)(2,1)S(1)}, bf16[512,512]{1,0:T(8,128)(2,1)S(1)}) custom-call(bf16[2,512]{1,0:T(2,128)(2,1)} %bitcast.1, s32[2,32]{1,0:T(2,128)} %labels_hbm.1, bf16[512,512]{1,0:T(8,128)(2,1)} %centres_hbm.1, bf16[512,512]{1,0:T(8,128)(2,1)} %momentum_hbm.1), custom_call_target="tpu_custom_call" | custom-call | tf_op jit(solution)/shard_map/pallas_call | solution.py:233
  17.2 1.0 %shard_map.68 = (f32[2,1,512]{2,1,0:T(1,128)}, bf16[512,512]{1,0:T(8,128)(2,1)}, bf16[512,512]{1,0:T(8,128)(2,1)}) custom-call(f32[2,1,512]{2,1,0:T(1,128)S(1)} %get-tuple-element.6.refs_0_, bf16[512,512]{1,0:T(8,128)(2,1)S(1)} %get-tuple-element.7.refs_1_, bf16[512,512]{1,0:T(8,128)(2,1)S(1)} %get-tuple-element.8.refs_2_), custom_call_target="tpu_custom_call" | custom-call | tf_op jit(solution)/shard_map/pallas_call | solution.py:259
